TPU v7x, 32 devices: a whole 2x2x4 slice. The times are simulated.
32 devices in a mesh: dp: 8 (over z, y), tp: 4 (over x, core).
Axes of the slice: x: 2, y: 2, z: 4, core: 2. Of those that a mesh axis runs over, the one named last changes fastest.
Arguments:
- tokens: bfloat16 [32, 1024, 768], P(('dp', 'tp')), may hold values from -11 to 11
- clip_lengths: int32 [32, 4], P(('dp', 'tp')), may hold values from 1 to 384, as said below
- out_grad: bfloat16 [32, 1024, 768], P(('dp', 'tp')), may hold values from -6 to 6
- w_query: bfloat16 [768, 768], P(('dp', 'tp')), may hold values from -0.21875 to 0.21875
- w_key: bfloat16 [768, 768], P(('dp', 'tp')), may hold values from -0.21875 to 0.21875
- w_value: bfloat16 [768, 768], P(('dp', 'tp')), may hold values from -0.21875 to 0.21875
- w_output: bfloat16 [768, 768], P(('dp', 'tp')), may hold values from -2.5 to 2.5
- gain_attention: bfloat16 [768], P(('dp', 'tp')), may hold values from 0.099609375 to 1.8984375
- gain_feed: bfloat16 [768], P(('dp', 'tp')), may hold values from 0.099609375 to 1.8984375
- w_expand: bfloat16 [768, 3072], P('dp', 'tp'), may hold values from -0.21875 to 0.21875
- w_reduce: bfloat16 [3072, 768], P('tp', 'dp'), may hold values from -0.4375 to 0.4375
Outputs:
- block_out: bfloat16 [32, 1024, 768], P(('dp', 'tp'))
- grad_tokens: float32 [32, 1024, 768], P(('dp', 'tp'))
- grad_w_query: float32 [768, 768], P(('dp', 'tp'))
- grad_w_key: float32 [768, 768], P(('dp', 'tp'))
- grad_w_value: float32 [768, 768], P(('dp', 'tp'))
- grad_w_output: float32 [768, 768], P(('dp', 'tp'))
- grad_gain_attention: float32 [768], P(('dp', 'tp'))
- grad_gain_feed: float32 [768], P(('dp', 'tp'))
- grad_w_expand: float32 [768, 3072], P('dp', 'tp')
- grad_w_reduce: float32 [3072, 768], P('tp', 'dp')
- root_mean_squares: float32 [3], replicated
Inputs may be any that keep to these rules, and one draw needn't show every extreme that they name: Each row of clip_lengths gives the lengths of its 3 clips in order, each at most 384 with one of exactly 384 in every row, then the number of padding slots at the row's end, 1 to 256; a row's entries sum to 1024.
All inputs are finite; a program needn't handle non-finite values.
Results may differ from a plain program's by a relative error of at most 0.015.
Values may be sent and summed in bfloat16 or wider, within the bound.
A program may use at most 192 MiB of HBM per device.

v0:
```python
from functools import partial
import jax
import jax.numpy as jnp
from jax import lax
from jax.sharding import PartitionSpec as P

HEADS = 12
HEAD_DIM = 64
SLOTS = 4


def segment_numbers(lengths, pack_len):
    clip_ends = jnp.cumsum(lengths[:, :-1], axis=-1, dtype=jnp.int32)
    position = jnp.arange(pack_len, dtype=jnp.int32)
    return jnp.sum(
        (position[None, :, None] >= clip_ends[:, None, :]).astype(jnp.int32),
        axis=-1,
        dtype=jnp.int32,
    )


def normalize(array_in):
    average = jnp.mean(array_in, axis=-1, keepdims=True)
    centred = array_in - average
    spread = jnp.mean(centred * centred, axis=-1, keepdims=True)
    inv_scale = lax.rsqrt(spread + 1e-06)
    return (centred * inv_scale, inv_scale)


def norm_back(grad_normed, unit_value, inv_scale, gain_vec):
    scaled = grad_normed * gain_vec
    inner_sum = (
        scaled
        - jnp.mean(scaled, axis=-1, keepdims=True)
        - unit_value * jnp.mean(scaled * unit_value, axis=-1, keepdims=True)
    )
    return (inv_scale * inner_sum, jnp.sum(grad_normed * unit_value, axis=0))


def dot_plain(left_side, right_side):
    return jnp.dot(left_side, right_side, preferred_element_type=jnp.float32)


def dot_first(left_side, right_side):
    return lax.dot_general(
        left_side, right_side, (((0,), (0,)), ((), ())), preferred_element_type=jnp.float32
    )


def dot_last(left_side, right_side):
    return lax.dot_general(
        left_side, right_side, (((1,), (1,)), ((), ())), preferred_element_type=jnp.float32
    )


def split_heads(array_in, rows_dev, pack_len):
    return (
        array_in.reshape(rows_dev, pack_len, HEADS, HEAD_DIM)
        .transpose(0, 2, 1, 3)
        .reshape(rows_dev * HEADS, pack_len, HEAD_DIM)
    )


def merge_heads(array_in, rows_dev, pack_len):
    return (
        array_in.reshape(rows_dev, HEADS, pack_len, HEAD_DIM)
        .transpose(0, 2, 1, 3)
        .reshape(rows_dev * pack_len, HEADS * HEAD_DIM)
    )


def head_scores(query_head, key_head, segments):
    same_clip = segments[:, None] == segments[None, :]
    scores = dot_last(query_head, key_head) * 0.125
    return jnp.where(same_clip, scores, -1e30)


def head_forward(block_item):
    query_head, key_head, value_head, segments = block_item
    scores = head_scores(query_head, key_head, segments)
    row_max = jnp.max(scores, axis=-1, keepdims=True)
    exponent = jnp.exp(scores - row_max)
    row_sum = jnp.sum(exponent, axis=-1, keepdims=True)
    weights = (exponent / row_sum).astype(jnp.bfloat16)
    return (dot_plain(weights, value_head).astype(jnp.bfloat16), row_max, row_sum)


def head_backward(block_item):
    query_head, key_head, value_head, segments, row_max, row_sum, grad_head = block_item
    scores = head_scores(query_head, key_head, segments)
    probabilities = jnp.exp(scores - row_max) / row_sum
    grad_probs = dot_last(grad_head, value_head)
    grad_value = dot_first(probabilities.astype(jnp.bfloat16), grad_head)
    inner_sum = jnp.sum(probabilities * grad_probs, axis=-1, keepdims=True)
    grad_scores = (probabilities * (grad_probs - inner_sum)).astype(jnp.bfloat16)
    grad_query = (dot_plain(grad_scores, key_head) * 0.125).astype(jnp.bfloat16)
    grad_key = (dot_first(grad_scores, query_head) * 0.125).astype(jnp.bfloat16)
    return (grad_query, grad_key, grad_value.astype(jnp.bfloat16))


def on_device(
    tokens,
    clip_lengths,
    out_grad,
    w_query,
    w_key,
    w_value,
    w_output,
    gain_attention,
    gain_feed,
    w_expand,
    w_reduce,
):
    rows_dev, pack_len, width = tokens.shape
    token_count = rows_dev * pack_len
    segments = segment_numbers(clip_lengths, pack_len)
    valid_rows = (segments < SLOTS - 1).astype(jnp.float32).reshape(-1)
    valid_column = valid_rows[:, None]
    inputs = tokens.reshape(token_count, width).astype(jnp.float32)
    query_full, key_full, value_full, output_full, gain_one, gain_two = (
        lax.all_gather(w_query, ("dp", "tp"), axis=0, tiled=True),
        lax.all_gather(w_key, ("dp", "tp"), axis=0, tiled=True),
        lax.all_gather(w_value, ("dp", "tp"), axis=0, tiled=True),
        lax.all_gather(w_output, ("dp", "tp"), axis=0, tiled=True),
        lax.all_gather(gain_attention, ("dp", "tp"), axis=0, tiled=True),
        lax.all_gather(gain_feed, ("dp", "tp"), axis=0, tiled=True),
    )
    expand_full, reduce_full = (
        lax.all_gather(w_expand, "dp", axis=0, tiled=True),
        lax.all_gather(w_reduce, "dp", axis=1, tiled=True),
    )
    gain_one = gain_one.astype(jnp.float32)
    gain_two = gain_two.astype(jnp.float32)
    unit_one, scale_one = normalize(inputs)
    normed = (unit_one * gain_one).astype(jnp.bfloat16)
    query_rows = dot_plain(normed, query_full).astype(jnp.bfloat16)
    key_rows = dot_plain(normed, key_full).astype(jnp.bfloat16)
    value_rows = dot_plain(normed, value_full).astype(jnp.bfloat16)
    head_segments = jnp.repeat(segments, HEADS, axis=0)
    query_heads = split_heads(query_rows, rows_dev, pack_len)
    key_heads = split_heads(key_rows, rows_dev, pack_len)
    value_heads = split_heads(value_rows, rows_dev, pack_len)
    mixed_heads, row_maxima, row_sums = lax.map(
        head_forward, (query_heads, key_heads, value_heads, head_segments)
    )
    mixed_rows = merge_heads(mixed_heads, rows_dev, pack_len)
    branch = dot_plain(mixed_rows, output_full)
    middle = inputs + branch
    unit_two, scale_two = normalize(middle)
    normed_feed = (unit_two * gain_two).astype(jnp.bfloat16)
    normed_rows = lax.all_gather(normed_feed, "tp", axis=0, tiled=True)
    hidden = dot_plain(normed_rows, expand_full)
    gelu_value, gelu_pull = jax.vjp(partial(jax.nn.gelu, approximate=False), hidden)
    active = gelu_value.astype(jnp.bfloat16)
    feed_out = lax.psum_scatter(
        dot_plain(
            lax.slice_in_dim(active, 0, token_count * lax.axis_size("tp"), axis=0), reduce_full
        ),
        "tp",
        scatter_dimension=0,
        tiled=True,
    )
    result = (middle + feed_out).astype(jnp.bfloat16).reshape(rows_dev, pack_len, width)
    totals_all = lax.psum(
        (
            jnp.sum(inputs * inputs * valid_column),
            jnp.sum(branch * branch * valid_column),
            jnp.sum(feed_out * feed_out * valid_column),
            jnp.sum(valid_rows),
        ),
        ("dp", "tp"),
    )
    rms_stats = jnp.sqrt(jnp.stack(totals_all[:3]) / (totals_all[3] * width))
    grad_result = out_grad.reshape(token_count, width).astype(jnp.float32) * valid_column
    grad_feed = grad_result.astype(jnp.bfloat16)
    grad_rows = lax.all_gather(grad_feed, "tp", axis=0, tiled=True)
    grad_reduce = dot_first(active, grad_rows)
    grad_active = dot_last(grad_rows, reduce_full)
    grad_hidden = gelu_pull(grad_active)[0].astype(jnp.bfloat16)
    grad_expand = dot_first(normed_rows, grad_hidden)
    grad_normed_feed = lax.psum_scatter(
        dot_last(grad_hidden, expand_full), "tp", scatter_dimension=0, tiled=True
    )
    grad_norm_two, grad_gain_two = norm_back(grad_normed_feed, unit_two, scale_two, gain_two)
    grad_middle = grad_result + grad_norm_two
    grad_branch = grad_middle.astype(jnp.bfloat16)
    grad_output_w = dot_first(mixed_rows, grad_branch)
    grad_mixed = dot_last(grad_branch, output_full).astype(jnp.bfloat16)
    grad_heads = split_heads(grad_mixed, rows_dev, pack_len)
    grad_query_heads, grad_key_heads, grad_value_heads = lax.map(
        head_backward,
        (query_heads, key_heads, value_heads, head_segments, row_maxima, row_sums, grad_heads),
    )
    grad_query = merge_heads(grad_query_heads, rows_dev, pack_len)
    grad_key = merge_heads(grad_key_heads, rows_dev, pack_len)
    grad_value = merge_heads(grad_value_heads, rows_dev, pack_len)
    grad_query_w = dot_first(normed, grad_query)
    grad_key_w = dot_first(normed, grad_key)
    grad_value_w = dot_first(normed, grad_value)
    grad_normed = (
        dot_last(grad_query, query_full)
        + dot_last(grad_key, key_full)
        + dot_last(grad_value, value_full)
    )
    grad_norm_one, grad_gain_one = norm_back(grad_normed, unit_one, scale_one, gain_one)
    grad_inputs = (grad_middle + grad_norm_one).reshape(rows_dev, pack_len, width)
    shard_expand, shard_reduce = (
        lax.psum_scatter(grad_expand, "dp", scatter_dimension=0, tiled=True),
        lax.psum_scatter(grad_reduce, "dp", scatter_dimension=1, tiled=True),
    )
    shard_query, shard_key, shard_value, shard_output, shard_gain_one, shard_gain_two = (
        lax.psum_scatter(grad_query_w, ("dp", "tp"), scatter_dimension=0, tiled=True),
        lax.psum_scatter(grad_key_w, ("dp", "tp"), scatter_dimension=0, tiled=True),
        lax.psum_scatter(grad_value_w, ("dp", "tp"), scatter_dimension=0, tiled=True),
        lax.psum_scatter(grad_output_w, ("dp", "tp"), scatter_dimension=0, tiled=True),
        lax.psum_scatter(grad_gain_one, ("dp", "tp"), scatter_dimension=0, tiled=True),
        lax.psum_scatter(grad_gain_two, ("dp", "tp"), scatter_dimension=0, tiled=True),
    )
    return (
        result,
        grad_inputs,
        shard_query,
        shard_key,
        shard_value,
        shard_output,
        shard_gain_one,
        shard_gain_two,
        shard_expand,
        shard_reduce,
        rms_stats,
    )


def solution(mesh):
    in_specs = (
        P(("dp", "tp"), None, None),
        P(("dp", "tp"), None),
        P(("dp", "tp"), None, None),
        P(("dp", "tp"), None),
        P(("dp", "tp"), None),
        P(("dp", "tp"), None),
        P(("dp", "tp"), None),
        P(("dp", "tp")),
        P(("dp", "tp")),
        P("dp", "tp"),
        P("tp", "dp"),
    )
    out_specs = (
        P(("dp", "tp"), None, None),
        P(("dp", "tp"), None, None),
        P(("dp", "tp"), None),
        P(("dp", "tp"), None),
        P(("dp", "tp"), None),
        P(("dp", "tp"), None),
        P(("dp", "tp")),
        P(("dp", "tp")),
        P("dp", "tp"),
        P("tp", "dp"),
        P(),
    )
    return jax.shard_map(
        on_device, mesh=mesh, in_specs=in_specs, out_specs=out_specs, check_vma=False
    )
```

profile of v0, /device:TPU:0, one launch (start us, length us, event | category | flops | bytes accessed | tf_op | source)
XLA Modules:
  0.0 1258.4 jit_solution(7682637012286789652)
XLA Ops:
  13.2 42.1 %all-reduce.5 = (bf16[768]{0:T(1024)(128)(2,1)S(1)}, bf16[768]{0:T(1024)(128)(2,1)S(1)}) all-reduce(bf16[768]{0:T(1024)(128)(2,1)S(1)} %dynamic-update-slice, bf16[768]{0:T(1024)(128)(2,1)S(1)} %dynamic-update-slice.1), channel_id=1, replica_groups=mesh['dp'=8,'tp'=4] {'dp','tp'}, use_global_device_ids=true, to_apply=%add | all-reduce | flops 1536 | bytes 6144
  56.0 11.7 all-gather.9.cloned.1.call-done
  73.3 50.4 %all-gather.11.cloned.1.call-done = bf16[768,768]{1,0:T(8,128)(2,1)} async-done(((bf16[24,768]{1,0:T(8,128)(2,1)}), bf16[768,768]{1,0:T(8,128)(2,1)}) %all-gather.11.cloned.1.call-update) | async-done | bytes 1179664 | tf_op jit(solution)/shard_map/all_gather | solution.py:122
  129.2 50.3 %all-gather.13.cloned.1.call-done = bf16[768,768]{1,0:T(8,128)(2,1)} async-done(((bf16[24,768]{1,0:T(8,128)(2,1)}), bf16[768,768]{1,0:T(8,128)(2,1)}) %all-gather.13.cloned.1.call-update) | async-done | bytes 1179664 | tf_op jit(solution)/shard_map/all_gather | solution.py:123
  185.4 68.7 %while.28 = (s32[]{:T(128)}, bf16[12,1024,64]{1,2,0:T(8,128)(2,1)S(1)}, f32[12,1024,1]{1,2,0:T(1,128)}, f32[12,1024,1]{1,2,0:T(1,128)}, s32[12,1024]{1,0:T(8,128...) while((s32[]{:T(128)}, ...), condition=%wide.region_7.8_spmd, body=%wide.region_4.7_spmd.sunk | while | flops 284227584 | bytes 13568109 | solution.py:143
  265.7 11.7 all-gather.19.cloned.1.call-done
  277.4 47.2 %all-gather.17.cloned.1.call-done = bf16[4096,768]{0,1:T(8,128)(2,1)} async-done(((bf16[1024,768]{0,1:T(8,128)(2,1)}), bf16[4096,768]{0,1:T(8,128)(2,1)}) %all-gather.17.cloned.1.call-update) | async-done | bytes 6291472 | tf_op jit(solution)/shard_map/all_gather | solution.py:151
  324.5 10.2 fusion.104
  334.7 33.1 %all-gather.21.cloned.1.call-done = bf16[768,768]{0,1:T(8,128)(2,1)} async-done(((bf16[768,96]{0,1:T(8,128)(2,1)}), bf16[768,768]{0,1:T(8,128)(2,1)}) %all-gather.21.cloned.1.call-update) | async-done | bytes 1179664 | tf_op jit(solution)/shard_map/all_gather | solution.py:130
  367.8 46.7 %all-gather.23.cloned.1.call-done = bf16[4096,768]{0,1:T(8,128)(2,1)} async-done(((bf16[1024,768]{0,1:T(8,128)(2,1)}), bf16[4096,768]{0,1:T(8,128)(2,1)}) %all-gather.23.cloned.1.call-update) | async-done | bytes 6291472 | tf_op jit(solution)/shard_map/all_gather | solution.py:176
  414.6 36.4 %add_convert_fusion = (bf16[4096,768]{1,0:T(8,128)(2,1)S(1)}, f32[4096,768]{1,0:T(8,128)}) fusion(f32[4096,768]{1,0:T(8,128)} %fusion.104, bf16[4096,768]{0,1:T(8,128)(2,1)} %all-gather.23.cloned.1.call-done, bf16[768,768]{0,1:T(8,128)(2,1)} %all-gather.21.cloned.1.call-done), kind=kOutput, calls=%fused_computation.64 | convolution fusion | flops 5058330624 | bytes 38928384 | tf_op jit(solution)/shard_map/dot_general | solution.py:51
  453.5 8.0 fusion.106
  461.6 11.3 multiply_convert_fusion.1
  476.6 7.9 fusion.105
  484.6 10.4 fusion.107
  495.1 10.1 fusion.110
  505.3 55.4 %reduce-scatter.11.cloned.1.call-done = f32[1024,768]{0,1:T(8,128)} async-done(((f32[4096,768]{0,1:T(8,128)}), f32[1024,768]{0,1:T(8,128)}) %reduce-scatter.11.cloned.1.call-update) | async-done | bytes 3145744 | tf_op jit(solution)/shard_map/reduce_scatter | solution.py:181
  563.6 98.6 %reduce-scatter.9.cloned.1.call-done = f32[1024,768]{0,1:T(8,128)} async-done(((f32[4096,768]{0,1:T(8,128)}), f32[1024,768]{0,1:T(8,128)}) %reduce-scatter.9.cloned.1.call-update) | async-done | bytes 3145744 | tf_op jit(solution)/shard_map/reduce_scatter | solution.py:155
  676.3 160.4 %while.29 = (s32[]{:T(128)}, bf16[12,1024,64]{1,2,0:T(8,128)(2,1)S(1)}, bf16[12,1024,64]{1,2,0:T(8,128)(2,1)}, bf16[12,1024,64]{1,2,0:T(8,128)(2,1)}, s32[12,102...) while((s32[]{:T(128)}, ...), condition=%wide.region_16.17_spmd, body=%wide.region_14.16_spmd.sunk | while | flops 682949632 | bytes 33739908 | solution.py:190
  870.8 39.8 %all-reduce.4 = (f32[768]{0:T(1024)S(1)}, f32[768]{0:T(1024)S(1)}, f32[1]{0:T(128)}, f32[1]{0:T(128)}, f32[1]{0:T(128)}, /*index=5*/f32[]{:T(128)}) all-reduce(f32[768]{0:T(1024)S(1)} %get-tuple-element.155, f32[768]{0:T(1024)S(1)} %get-tuple-element.153, f32[1]{0:T(128)} %bitcast.60, ...), channel_id=8, replica_groups=mesh['dp'=8,'tp'=4] {'dp','tp'}, use_global_device_ids=true, to_apply=%region_24.25.clone | all-reduce | flops 1540 | bytes 12320
  914.8 23.9 %reduce-scatter.13.cloned.1.call-done = f32[24,768]{1,0:T(8,128)} async-done(((f32[768,768]{1,0:T(8,128)}), f32[24,768]{1,0:T(8,128)}) %reduce-scatter.13.cloned.1.call-update) | async-done | bytes 73744 | tf_op jit(solution)/shard_map/reduce_scatter | solution.py:212
  938.7 104.6 %reduce-scatter.15.cloned.1.call-done = f32[24,768]{1,0:T(8,128)} async-done(((f32[768,768]{1,0:T(8,128)}), f32[24,768]{1,0:T(8,128)}) %reduce-scatter.15.cloned.1.call-update) | async-done | bytes 73744 | tf_op jit(solution)/shard_map/reduce_scatter | solution.py:213
  1043.3 103.7 %reduce-scatter.17.cloned.1.call-done = f32[24,768]{1,0:T(8,128)} async-done(((f32[768,768]{1,0:T(8,128)}), f32[24,768]{1,0:T(8,128)}) %reduce-scatter.17.cloned.1.call-update) | async-done | bytes 73744 | tf_op jit(solution)/shard_map/reduce_scatter | solution.py:214
  1147.0 104.7 %reduce-scatter.19.cloned.1.call-done = f32[24,768]{1,0:T(8,128)} async-done(((f32[768,768]{1,0:T(8,128)}), f32[24,768]{1,0:T(8,128)}) %reduce-scatter.19.cloned.1.call-update) | async-done | bytes 73744 | tf_op jit(solution)/shard_map/reduce_scatter | solution.py:215
  (328 shorter events, 324.4 us)
Async XLA Ops:
  7.2 60.6 %all-gather.9.cloned.1.call-start = ((), (), s32[]{:S(2)}) async-start(), calls=%async_computation.8 | async-start | bytes 1216512 | tf_op jit(solution)/shard_map/all_gather | solution.py:121
  7.9 115.7 %all-gather.11.cloned.1.call-start = ((), (), s32[]{:S(2)}) async-start(), calls=%async_computation.9 | async-start | bytes 1216512 | tf_op jit(solution)/shard_map/all_gather | solution.py:122
  8.7 170.9 %all-gather.13.cloned.1.call-start = ((), (), s32[]{:S(2)}) async-start(), calls=%async_computation.10 | async-start | bytes 1216512 | tf_op jit(solution)/shard_map/all_gather | solution.py:123
  9.4 244.7 %all-gather.15.cloned.1.call-start = ((), (), s32[]{:S(2)}) async-start(), calls=%async_computation.11 | async-start | bytes 1216512 | tf_op jit(solution)/shard_map/all_gather | solution.py:124
  10.0 267.4 %all-gather.19.cloned.1.call-start = ((), (), s32[]{:S(2)}) async-start(), calls=%async_computation.13 | async-start | bytes 1327104 | tf_op jit(solution)/shard_map/all_gather | solution.py:129
  10.6 314.0 %all-gather.17.cloned.1.call-start = ((), (), s32[]{:S(2)}) async-start(), calls=%async_computation.12 | async-start | bytes 7864320 | tf_op jit(solution)/shard_map/all_gather | solution.py:151
  12.4 241.8 %copy-start.2 = (bf16[1,1024,768]{1,2,0:T(8,128)(2,1)}, bf16[1,1024,768]{1,2,0:T(8,128)(2,1)S(1)}, u32[]{:S(2)}) copy-start(bf16[1,1024,768]{1,2,0:T(8,128)(2,1)S(1)} %copy.42) | copy-start | bytes 4718596
  12.7 251.3 %copy-start.19 = (s32[1024]{0:T(1024)}, s32[1024]{0:T(1024)S(1)}, u32[]{:S(2)}) copy-start(s32[1024]{0:T(1024)S(1)} %fusion.89) | copy-start | bytes 12292
  56.0 203.5 %copy-start.21 = (f32[768]{0:T(1024)}, f32[768]{0:T(1024)S(1)}, u32[]{:S(2)}) copy-start(f32[768]{0:T(1024)S(1)} %convert_element_type.111) | copy-start | bytes 9220
  262.4 105.5 %all-gather.21.cloned.1.call-start = ((), (), s32[]{:S(2)}) async-start(), calls=%async_computation.14 | async-start | bytes 1327104 | tf_op jit(solution)/shard_map/all_gather | solution.py:130
  263.1 151.4 %all-gather.23.cloned.1.call-start = ((), (), s32[]{:S(2)}) async-start(), calls=%async_computation.16 | async-start | bytes 7864320 | tf_op jit(solution)/shard_map/all_gather | solution.py:176
  265.6 295.1 %reduce-scatter.11.cloned.1.call-start = ((), (), s32[]{:S(2)}) async-start(), calls=%async_computation.17 | async-start | bytes 15728640 | tf_op jit(solution)/shard_map/reduce_scatter | solution.py:181
  461.5 200.7 %reduce-scatter.9.cloned.1.call-start = ((), (), s32[]{:S(2)}) async-start(), calls=%async_computation.15 | async-start | bytes 15728640 | tf_op jit(solution)/shard_map/reduce_scatter | solution.py:155
  484.6 430.2 %reduce-scatter.21.cloned.1.call-start = ((), (), s32[]{:S(2)}) async-start(), calls=%async_computation.22 | async-start | bytes 2654208 | tf_op jit(solution)/shard_map/reduce_scatter | solution.py:208
  495.1 419.7 %reduce-scatter.23.cloned.1.call-start = ((), (), s32[]{:S(2)}) async-start(), calls=%async_computation.23 | async-start | bytes 2654208 | tf_op jit(solution)/shard_map/reduce_scatter | solution.py:209
  505.3 157.0 %copy-start.28 = (f32[1024]{0:T(1024)S(1)}, f32[1024]{0:T(1024)}, u32[]{:S(2)}) copy-start(f32[1024]{0:T(1024)} %copy-done.27) | copy-start | bytes 12292
  505.3 433.4 %reduce-scatter.13.cloned.1.call-start = ((), (), s32[]{:S(2)}) async-start(), calls=%async_computation.18 | async-start | bytes 2433024 | tf_op jit(solution)/shard_map/reduce_scatter | solution.py:212
  676.3 160.4 %copy-start.3 = (bf16[1,1024,768]{1,2,0:T(8,128)(2,1)S(1)}, bf16[1,1024,768]{1,2,0:T(8,128)(2,1)}, u32[]{:S(2)}) copy-start(bf16[1,1024,768]{1,2,0:T(8,128)(2,1)} %copy-done.2) | copy-start | bytes 4718596
  676.3 160.4 %copy-start.26 = (f32[1024]{0:T(1024)S(1)}, f32[1024]{0:T(1024)}, u32[]{:S(2)}) copy-start(f32[1024]{0:T(1024)} %copy-done.25) | copy-start | bytes 12292
  676.3 160.4 %copy-start.30 = (f32[768]{0:T(1024)S(1)}, f32[768]{0:T(1024)}, u32[]{:S(2)}) copy-start(f32[768]{0:T(1024)} %copy-done.29) | copy-start | bytes 9220
  676.3 160.4 %copy-start.32 = (f32[1024]{0:T(1024)S(1)}, f32[1024]{0:T(1024)}, u32[]{:S(2)}) copy-start(f32[1024]{0:T(1024)} %copy-done.31) | copy-start | bytes 12292
  839.6 203.7 %reduce-scatter.15.cloned.1.call-start = ((), (), s32[]{:S(2)}) async-start(), calls=%async_computation.19 | async-start | bytes 2433024 | tf_op jit(solution)/shard_map/reduce_scatter | solution.py:213
  844.0 303.0 %reduce-scatter.17.cloned.1.call-start = ((), (), s32[]{:S(2)}) async-start(), calls=%async_computation.20 | async-start | bytes 2433024 | tf_op jit(solution)/shard_map/reduce_scatter | solution.py:214
  848.6 403.1 %reduce-scatter.19.cloned.1.call-start = ((), (), s32[]{:S(2)}) async-start(), calls=%async_computation.21 | async-start | bytes 2433024 | tf_op jit(solution)/shard_map/reduce_scatter | solution.py:215
  (33 other events, 985.0 us)
Sparse Core Ops, SparseCore 0:
  10.9 56.7 all-gather.8
  70.7 52.9 all-gather.10
  126.6 52.9 all-gather.12
  182.3 52.9 all-gather.14
  237.4 39.9 all-gather.18
  279.4 45.1 all-gather.16
  326.7 41.0 all-gather.20
  369.4 45.1 all-gather.22
  461.6 99.0 reduce-scatter.10
  563.2 99.0 reduce-scatter.8
  666.3 68.9 reduce-scatter.20
  739.3 68.2 reduce-scatter.22
  839.7 98.9 reduce-scatter.12
  945.3 97.9 reduce-scatter.14
  1049.1 97.9 reduce-scatter.16
  1153.6 98.0 reduce-scatter.18
where the time goes:
time: 1270 us; the launch traced here: 1260 us
  waiting for transfers between devices  746 us (59%)
  matrix products  299 us (24%)
  blocking collectives  81.8 us (6%)
  local copies, waits for them, and re-layouts  57.7 us (5%)
  other arithmetic  57.1 us (4%)
  between operations  15.3 us (1%)
    dot_general x42, matrix products, dot_last(): lax.dot_general(left_side, right_side, (((1,), (1,)), ((), ())), preferre...  128 us
    reduce_scatter x1, waiting for transfers between devices, on_device(): lax.psum_scatter(grad_output_w, ('dp', 'tp'), scatter_dimension=0, tiled=...  105 us
    reduce_scatter x1, waiting for transfers between devices, on_device(): lax.psum_scatter(grad_key_w, ('dp', 'tp'), scatter_dimension=0, tiled=True)  105 us
    reduce_scatter x1, waiting for transfers between devices, on_device(): lax.psum_scatter(grad_value_w, ('dp', 'tp'), scatter_dimension=0, tiled=T...  104 us
    reduce_scatter x1, waiting for transfers between devices, on_device(): lax.psum_scatter(dot_plain(lax.slice_in_dim(active, 0, token_count * lax....  98.6 us
    dot_general x30, matrix products, dot_first(): lax.dot_general(left_side, right_side, (((0,), (0,)), ((), ())), preferre...  94.1 us
    unnamed x2, blocking collectives  81.8 us
    dot_general x30, matrix products, dot_plain(): return jnp.dot(left_side, right_side, preferred_element_type=jnp.float32)  76.9 us
  transfers between devices with their start and end apart: 16, of which 13 were waited for; matrix products, arithmetic and copies ran while one was open for 29% of the time, Pallas kernels for 0%

commit v1 on v0

--- a/solution.py
+++ b/solution.py
@@ -7,6 +7,12 @@
 HEADS = 12
 HEAD_DIM = 64
 SLOTS = 4
+
+
+def fill_sector_now(slab_in, row_dim):
+    z = list(slab_in.shape[1:])
+    z[row_dim] *= slab_in.shape[0]
+    return jnp.moveaxis(slab_in, 0, row_dim).reshape(z)
 
 
 def segment_numbers(lengths, pack_len):
@@ -125,9 +131,28 @@
         lax.all_gather(gain_attention, ("dp", "tp"), axis=0, tiled=True),
         lax.all_gather(gain_feed, ("dp", "tp"), axis=0, tiled=True),
     )
+
+    def match_table(m, which_axis, along_dim):
+        n_dev_all = lax.axis_size(which_axis)
+        nodes = tuple(((src_i, (src_i + 1) % n_dev_all) for src_i in range(n_dev_all)))
+        fields = tuple(((t, dev_i) for dev_i, t in nodes))
+        near, after = ([], [])
+        for it in range(n_dev_all - 1):
+            if it % 2 == 0:
+                near.append(lax.ppermute(near[-1] if near else m, axis_name=which_axis, perm=nodes))
+            else:
+                after.append(
+                    lax.ppermute(after[-1] if after else m, axis_name=which_axis, perm=fields)
+                )
+        new = jnp.stack([*near[::-1], m, *after])
+        v_next = lax.axis_index(which_axis)
+        earlier = v_next - len(near)
+        new = new[(jnp.arange(n_dev_all) - earlier) % n_dev_all]
+        return fill_sector_now(new, along_dim)
+
     expand_full, reduce_full = (
         lax.all_gather(w_expand, "dp", axis=0, tiled=True),
-        lax.all_gather(w_reduce, "dp", axis=1, tiled=True),
+        match_table(w_reduce, which_axis="dp", along_dim=1),
     )
     gain_one = gain_one.astype(jnp.float32)
     gain_two = gain_two.astype(jnp.float32)

time: 1270 us -> 1230 us (0.969)
  waiting for transfers between devices: 746 us -> 688 us
  starting transfers between devices: 0.64 us -> 17.2 us
    all_gather x1 -> x0, waiting for transfers between devices: 33.1 us -> none  [on_device(): lax.all_gather(w_reduce, 'dp', axis=1, tiled=True)]
    all_gather x1, waiting for transfers between devices: 47.2 us -> 24.6 us  [on_device(): normed_rows = lax.all_gather(normed_feed, 'tp', axis=0, tiled=True)]
    ppermute x0 -> x7, waiting for transfers between devices: none -> 19.1 us  [the longest x4 18.3 us: match_table(): lax.ppermute(near[-1] if near else m, axis_name=which_axis, perm=nodes)]
    ppermute x0 -> x7, starting transfers between devices: none -> 16.6 us  [the longest x3 13.2 us: match_table(): lax.ppermute(after[-1] if after else m, axis_name=which_axis, perm=fields)]
  transfers between devices with their start and end apart: 16 -> 22, of which waited for: 13 -> 16; matrix products, arithmetic and copies ran while one was open for 29% -> 30% of each run, Pallas kernels for 0% -> 0%
where the time goes in v1:
time: 1230 us; the launch traced here: 1220 us
  waiting for transfers between devices  688 us (56%)
  matrix products  299 us (24%)
  blocking collectives  81.9 us (7%)
  local copies, waits for them, and re-layouts  58.6 us (5%)
  other arithmetic  57.1 us (5%)
  starting transfers between devices  17.2 us (1%)
  between operations  15.4 us (1%)
    dot_general x42, matrix products, dot_last(): lax.dot_general(left_side, right_side, (((1,), (1,)), ((), ())), preferre...  128 us
    reduce_scatter x1, waiting for transfers between devices, on_device(): lax.psum_scatter(grad_key_w, ('dp', 'tp'), scatter_dimension=0, tiled=True)  105 us
    reduce_scatter x1, waiting for transfers between devices, on_device(): lax.psum_scatter(grad_output_w, ('dp', 'tp'), scatter_dimension=0, tiled=...  105 us
    reduce_scatter x1, waiting for transfers between devices, on_device(): lax.psum_scatter(grad_value_w, ('dp', 'tp'), scatter_dimension=0, tiled=T...  104 us
    reduce_scatter x1, waiting for transfers between devices, on_device(): lax.psum_scatter(dot_plain(lax.slice_in_dim(active, 0, token_count * lax....  98.8 us
    dot_general x30, matrix products, dot_first(): lax.dot_general(left_side, right_side, (((0,), (0,)), ((), ())), preferre...  94.2 us
    unnamed x2, blocking collectives  81.9 us
    dot_general x30, matrix products, dot_plain(): return jnp.dot(left_side, right_side, preferred_element_type=jnp.float32)  77.2 us
  transfers between devices with their start and end apart: 22, of which 16 were waited for; matrix products, arithmetic and copies ran while one was open for 30% of the time, Pallas kernels for 0%

profile of v1, /device:TPU:0, one launch (start us, length us, event | category | flops | bytes accessed | tf_op | source)
XLA Modules:
  0.0 1218.5 jit_solution(11331401852950997089)
XLA Ops:
  13.2 42.1 %all-reduce.5 = (bf16[768]{0:T(1024)(128)(2,1)S(1)}, bf16[768]{0:T(1024)(128)(2,1)S(1)}) all-reduce(bf16[768]{0:T(1024)(128)(2,1)S(1)} %dynamic-update-slice, bf16[768]{0:T(1024)(128)(2,1)S(1)} %dynamic-update-slice.1), channel_id=1, replica_groups=mesh['dp'=8,'tp'=4] {'dp','tp'}, use_global_device_ids=true, to_apply=%add | all-reduce | flops 1536 | bytes 6144
  56.0 11.7 all-gather.8.cloned.1.call-done
  73.3 50.4 %all-gather.10.cloned.1.call-done = bf16[768,768]{1,0:T(8,128)(2,1)} async-done(((bf16[24,768]{1,0:T(8,128)(2,1)}), bf16[768,768]{1,0:T(8,128)(2,1)}) %all-gather.10.cloned.1.call-update) | async-done | bytes 1179664 | tf_op jit(solution)/shard_map/all_gather | solution.py:128
  129.2 50.3 %all-gather.12.cloned.1.call-done = bf16[768,768]{1,0:T(8,128)(2,1)} async-done(((bf16[24,768]{1,0:T(8,128)(2,1)}), bf16[768,768]{1,0:T(8,128)(2,1)}) %all-gather.12.cloned.1.call-update) | async-done | bytes 1179664 | tf_op jit(solution)/shard_map/all_gather | solution.py:129
  185.3 68.7 %while.28 = (s32[]{:T(128)}, bf16[12,1024,64]{1,2,0:T(8,128)(2,1)S(1)}, f32[12,1024,1]{1,2,0:T(1,128)}, f32[12,1024,1]{1,2,0:T(1,128)}, s32[12,1024]{1,0:T(8,128...) while((s32[]{:T(128)}, ...), condition=%wide.region_7.8_spmd, body=%wide.region_4.7_spmd.sunk | while | flops 284227584 | bytes 13568109 | solution.py:168
  266.9 8.9 collective-permute-done
  301.7 24.6 %all-gather.16.cloned.1.call-done = bf16[4096,768]{0,1:T(8,128)(2,1)} async-done(((bf16[1024,768]{0,1:T(8,128)(2,1)}), bf16[4096,768]{0,1:T(8,128)(2,1)}) %all-gather.16.cloned.1.call-update) | async-done | bytes 6291472 | tf_op jit(solution)/shard_map/all_gather | solution.py:176
  326.3 10.5 fusion.106
  336.8 37.5 %all-gather.20.cloned.1.call-done = bf16[4096,768]{0,1:T(8,128)(2,1)} async-done(((bf16[1024,768]{0,1:T(8,128)(2,1)}), bf16[4096,768]{0,1:T(8,128)(2,1)}) %all-gather.20.cloned.1.call-update) | async-done | bytes 6291472 | tf_op jit(solution)/shard_map/all_gather | solution.py:201
  374.3 36.2 %add_convert_fusion = (bf16[4096,768]{1,0:T(8,128)(2,1)S(1)}, f32[4096,768]{1,0:T(8,128)}) fusion(f32[4096,768]{1,0:T(8,128)} %fusion.106, bf16[4096,768]{0,1:T(8,128)(2,1)} %all-gather.20.cloned.1.call-done, bf16[768,768]{0,1:T(8,128)(2,1)S(1)} %bitcast.256), kind=kOutput, calls=%fused_computation.65 | convolution fusion | flops 5058330624 | bytes 38928384 | tf_op jit(solution)/shard_map/dot_general | solution.py:57
  413.1 7.9 fusion.108
  421.1 11.1 multiply_convert_fusion.1
  436.0 7.9 fusion.107
  444.1 10.4 fusion.109
  454.5 10.1 fusion.112
  464.7 55.5 %reduce-scatter.11.cloned.1.call-done = f32[1024,768]{0,1:T(8,128)} async-done(((f32[4096,768]{0,1:T(8,128)}), f32[1024,768]{0,1:T(8,128)}) %reduce-scatter.11.cloned.1.call-update) | async-done | bytes 3145744 | tf_op jit(solution)/shard_map/reduce_scatter | solution.py:206
  523.2 98.8 %reduce-scatter.9.cloned.1.call-done = f32[1024,768]{0,1:T(8,128)} async-done(((f32[4096,768]{0,1:T(8,128)}), f32[1024,768]{0,1:T(8,128)}) %reduce-scatter.9.cloned.1.call-update) | async-done | bytes 3145744 | tf_op jit(solution)/shard_map/reduce_scatter | solution.py:180
  622.0 6.7 multiply_reduce_fusion.2
  636.0 160.3 %while.29 = (s32[]{:T(128)}, bf16[12,1024,64]{1,2,0:T(8,128)(2,1)S(1)}, bf16[12,1024,64]{1,2,0:T(8,128)(2,1)}, bf16[12,1024,64]{1,2,0:T(8,128)(2,1)}, s32[12,102...) while((s32[]{:T(128)}, ...), condition=%wide.region_16.17_spmd, body=%wide.region_14.16_spmd.sunk | while | flops 682949632 | bytes 33739908 | solution.py:215
  830.5 39.8 %all-reduce.4 = (f32[768]{0:T(1024)S(1)}, f32[768]{0:T(1024)S(1)}, f32[1]{0:T(128)}, f32[1]{0:T(128)}, f32[1]{0:T(128)}, /*index=5*/f32[]{:T(128)}) all-reduce(f32[768]{0:T(1024)S(1)} %get-tuple-element.155, f32[768]{0:T(1024)S(1)} %get-tuple-element.153, f32[1]{0:T(128)} %bitcast.72, ...), channel_id=8, replica_groups=mesh['dp'=8,'tp'=4] {'dp','tp'}, use_global_device_ids=true, to_apply=%region_24.25.clone | all-reduce | flops 1540 | bytes 12320
  874.7 23.9 %reduce-scatter.13.cloned.1.call-done = f32[24,768]{1,0:T(8,128)} async-done(((f32[768,768]{1,0:T(8,128)}), f32[24,768]{1,0:T(8,128)}) %reduce-scatter.13.cloned.1.call-update) | async-done | bytes 73744 | tf_op jit(solution)/shard_map/reduce_scatter | solution.py:237
  898.6 104.8 %reduce-scatter.15.cloned.1.call-done = f32[24,768]{1,0:T(8,128)} async-done(((f32[768,768]{1,0:T(8,128)}), f32[24,768]{1,0:T(8,128)}) %reduce-scatter.15.cloned.1.call-update) | async-done | bytes 73744 | tf_op jit(solution)/shard_map/reduce_scatter | solution.py:238
  1003.4 103.8 %reduce-scatter.17.cloned.1.call-done = f32[24,768]{1,0:T(8,128)} async-done(((f32[768,768]{1,0:T(8,128)}), f32[24,768]{1,0:T(8,128)}) %reduce-scatter.17.cloned.1.call-update) | async-done | bytes 73744 | tf_op jit(solution)/shard_map/reduce_scatter | solution.py:239
  1107.2 104.6 %reduce-scatter.19.cloned.1.call-done = f32[24,768]{1,0:T(8,128)} async-done(((f32[768,768]{1,0:T(8,128)}), f32[24,768]{1,0:T(8,128)}) %reduce-scatter.19.cloned.1.call-update) | async-done | bytes 73744 | tf_op jit(solution)/shard_map/reduce_scatter | solution.py:240
  (350 shorter events, 344.9 us)
Async XLA Ops:
  7.2 60.6 %all-gather.8.cloned.1.call-start = ((), (), s32[]{:S(2)}) async-start(), calls=%async_computation.8 | async-start | bytes 1216512 | tf_op jit(solution)/shard_map/all_gather | solution.py:127
  7.9 115.7 %all-gather.10.cloned.1.call-start = ((), (), s32[]{:S(2)}) async-start(), calls=%async_computation.9 | async-start | bytes 1216512 | tf_op jit(solution)/shard_map/all_gather | solution.py:128
  8.7 170.9 %all-gather.12.cloned.1.call-start = ((), (), s32[]{:S(2)}) async-start(), calls=%async_computation.10 | async-start | bytes 1216512 | tf_op jit(solution)/shard_map/all_gather | solution.py:129
  9.4 244.7 %all-gather.14.cloned.1.call-start = ((), (), s32[]{:S(2)}) async-start(), calls=%async_computation.11 | async-start | bytes 1216512 | tf_op jit(solution)/shard_map/all_gather | solution.py:130
  10.0 291.7 %all-gather.18.cloned.1.call-start = ((), (), s32[]{:S(2)}) async-start(), calls=%async_computation.13 | async-start | bytes 1327104 | tf_op jit(solution)/shard_map/all_gather | solution.py:154
  10.6 315.7 %all-gather.16.cloned.1.call-start = ((), (), s32[]{:S(2)}) async-start(), calls=%async_computation.12 | async-start | bytes 7864320 | tf_op jit(solution)/shard_map/all_gather | solution.py:176
  12.4 241.8 %copy-start.2 = (bf16[1,1024,768]{1,2,0:T(8,128)(2,1)}, bf16[1,1024,768]{1,2,0:T(8,128)(2,1)S(1)}, u32[]{:S(2)}) copy-start(bf16[1,1024,768]{1,2,0:T(8,128)(2,1)S(1)} %copy.42) | copy-start | bytes 4718596
  12.7 250.7 %copy-start.20 = (s32[1024]{0:T(1024)}, s32[1024]{0:T(1024)S(1)}, u32[]{:S(2)}) copy-start(s32[1024]{0:T(1024)S(1)} %fusion.89) | copy-start | bytes 12292
  262.4 111.9 %all-gather.20.cloned.1.call-start = ((), (), s32[]{:S(2)}) async-start(), calls=%async_computation.15 | async-start | bytes 7864320 | tf_op jit(solution)/shard_map/all_gather | solution.py:201
  265.1 255.2 %reduce-scatter.11.cloned.1.call-start = ((), (), s32[]{:S(2)}) async-start(), calls=%async_computation.16 | async-start | bytes 15728640 | tf_op jit(solution)/shard_map/reduce_scatter | solution.py:206
  265.1 10.6 collective-permute-start
  275.8 8.5 collective-permute-start.1
  275.8 9.2 collective-permute-start.4
  284.3 7.9 collective-permute-start.2
  284.9 8.4 collective-permute-start.5
  292.2 7.9 collective-permute-start.3
  293.3 7.7 collective-permute-start.6
  421.1 200.9 %reduce-scatter.9.cloned.1.call-start = ((), (), s32[]{:S(2)}) async-start(), calls=%async_computation.14 | async-start | bytes 15728640 | tf_op jit(solution)/shard_map/reduce_scatter | solution.py:180
  444.0 430.7 %reduce-scatter.21.cloned.1.call-start = ((), (), s32[]{:S(2)}) async-start(), calls=%async_computation.21 | async-start | bytes 2654208 | tf_op jit(solution)/shard_map/reduce_scatter | solution.py:233
  454.5 420.2 %reduce-scatter.23.cloned.1.call-start = ((), (), s32[]{:S(2)}) async-start(), calls=%async_computation.22 | async-start | bytes 2654208 | tf_op jit(solution)/shard_map/reduce_scatter | solution.py:234
  464.7 433.9 %reduce-scatter.13.cloned.1.call-start = ((), (), s32[]{:S(2)}) async-start(), calls=%async_computation.17 | async-start | bytes 2433024 | tf_op jit(solution)/shard_map/reduce_scatter | solution.py:237
  799.2 204.2 %reduce-scatter.15.cloned.1.call-start = ((), (), s32[]{:S(2)}) async-start(), calls=%async_computation.18 | async-start | bytes 2433024 | tf_op jit(solution)/shard_map/reduce_scatter | solution.py:238
  803.6 303.6 %reduce-scatter.17.cloned.1.call-start = ((), (), s32[]{:S(2)}) async-start(), calls=%async_computation.19 | async-start | bytes 2433024 | tf_op jit(solution)/shard_map/reduce_scatter | solution.py:239
  808.2 403.5 %reduce-scatter.19.cloned.1.call-start = ((), (), s32[]{:S(2)}) async-start(), calls=%async_computation.20 | async-start | bytes 2433024 | tf_op jit(solution)/shard_map/reduce_scatter | solution.py:240
  (39 other events, 1791.0 us)
Sparse Core Ops, SparseCore 0:
  10.9 56.7 all-gather.7
  70.7 52.9 all-gather.9
  126.6 52.9 all-gather.11
  182.3 52.9 all-gather.13
  237.3 40.5 all-gather.17
  279.9 46.3 all-gather.15
  327.9 46.3 all-gather.19
  421.2 99.0 reduce-scatter.10
  522.9 99.0 reduce-scatter.8
  625.9 68.9 reduce-scatter.20
  699.0 68.0 reduce-scatter.22
  799.3 99.2 reduce-scatter.12
  905.3 98.0 reduce-scatter.14
  1009.1 97.9 reduce-scatter.16
  1113.7 97.9 reduce-scatter.18
